TPU v7x, 32 devices: a whole 2x2x4 slice. The times are simulated.
32 devices in a mesh: fsdp: 8 (over y, x, core), ep: 4 (over z).
Axes of the slice: x: 2, y: 2, z: 4, core: 2. Of those that a mesh axis runs over, the one named last changes fastest.
Arguments:
- hidden: bfloat16 [2048, 8192], P('fsdp', 'ep'), may hold values from -6 to 6
- w_down: bfloat16 [6144, 2, 8192], P('fsdp', None, 'ep'), may hold values from -0.0625 to 0.0625
- route_ids: int32 [1024, 2], P('fsdp'), may hold values from 0 to 7, as said below
- probs: float32 [1024, 2], P('fsdp'), may hold values from 0.1 to 0.9
- grad_out: bfloat16 [1024, 6144], P('fsdp', 'ep'), may hold values from -6 to 6
Outputs:
- output: bfloat16 [1024, 6144], P('fsdp', 'ep')
- grad_hidden: bfloat16 [2048, 8192], P('fsdp', 'ep')
- grad_weight: bfloat16 [6144, 2, 8192], P('fsdp', None, 'ep')
- grad_probs: float32 [1024, 2], P('fsdp')
Inputs may be any that keep to these rules, and one draw needn't show every extreme that they name: `route_ids`: each token names 2 different experts. Within one panel's 128 tokens, experts 0 and 1 are each named by 1 to 128 tokens, and in some panel both are named by all 128 tokens.
All inputs are finite; a program needn't handle non-finite values.
Results may differ from a plain program's by a relative error of at most 0.012.
Values may be sent and summed in bfloat16 or wider, within the bound.
A program may use at most 384 MiB of HBM per device.

v0:
```python
import jax
import jax.numpy as jnp
from jax import lax
from jax.sharding import PartitionSpec as P

BLOCK = 128


def route_layout(route_part, prob_part, expert_count, block_rows, row_count):
    token_count = route_part.shape[0]
    experts = jnp.arange(expert_count, dtype=jnp.int32)
    hits = (route_part[:, :, None] == experts[None, None, :]).astype(jnp.int32)
    named = jnp.sum(hits, axis=1)
    counts = jnp.sum(named, axis=0)
    ranks = jnp.cumsum(named, axis=0) - named
    padded = (counts + block_rows - 1) // block_rows * block_rows
    offsets = jnp.cumsum(padded) - padded
    row_of = jnp.sum(hits * (offsets[None, None, :] + ranks[:, None, :]), axis=2)
    valid = jnp.sum(hits, axis=2)
    starts = jnp.arange(row_count // block_rows, dtype=jnp.int32) * block_rows
    inside = (starts[:, None] >= offsets[None, :]) & (starts[:, None] < (offsets + padded)[None, :])
    block_exp = jnp.sum(jnp.where(inside, experts[None, :] + 1, 0), axis=1) - 1
    target = jnp.where(valid > 0, row_of, row_count).reshape(-1)
    token_index = jnp.broadcast_to(
        jnp.arange(token_count, dtype=jnp.int32)[:, None], route_part.shape
    ).reshape(-1)
    row_tok = jnp.zeros((row_count,), jnp.int32).at[target].set(token_index, mode="drop")
    row_live = (
        jnp.zeros((row_count,), jnp.int32).at[target].set(jnp.ones_like(token_index), mode="drop")
    )
    row_prob = (
        jnp.zeros((row_count,), prob_part.dtype).at[target].set(prob_part.reshape(-1), mode="drop")
    )
    return (row_of, valid, block_exp, row_tok, row_live, row_prob)


def local(hidden, w_down, route_ids, probs, grad_out):
    row_count, unit_count = hidden.shape
    expert_count = w_down.shape[1]
    block_count = row_count // BLOCK
    row_of, valid, block_exp, row_tok, row_live, row_prob = route_layout(
        route_ids, probs, expert_count, BLOCK, row_count
    )
    safe_exp = jnp.maximum(block_exp, 0)
    prob_valid = probs * valid.astype(jnp.float32)
    full_grads = lax.all_gather(grad_out, "ep", axis=1, tiled=True)
    model_width = full_grads.shape[1]
    routed = jnp.where(row_live[:, None] > 0, full_grads[row_tok], jnp.zeros((), jnp.bfloat16))
    scaled = (row_prob[:, None] * routed.astype(jnp.float32)).astype(jnp.bfloat16)
    hid_blocks = hidden.reshape(block_count, BLOCK, unit_count)
    routed_blocks = routed.reshape(block_count, BLOCK, model_width)
    row_exp = jnp.repeat(block_exp, BLOCK)
    member = (row_exp[:, None] == jnp.arange(expert_count, dtype=jnp.int32)[None, :]).astype(
        jnp.bfloat16
    )
    masked_hid = hidden[:, None, :] * member[:, :, None]
    piece = lax.all_gather(w_down, "fsdp", axis=0, tiled=True)
    width = piece.shape[0]
    chosen = jnp.take(piece, safe_exp, axis=1)
    out_rows = jnp.einsum(
        "bri,dbi->brd", hid_blocks, chosen, preferred_element_type=jnp.float32
    ).reshape(row_count, width)
    back_total = jnp.einsum(
        "brd,dbi->bri", routed_blocks, chosen, preferred_element_type=jnp.float32
    )
    combined = jnp.sum(prob_valid[:, :, None] * out_rows[row_of], axis=1)
    out_total = combined
    out_total, back_total = (out_total, back_total)
    grad_weight = lax.psum_scatter(
        jnp.einsum("rd,rei->dei", scaled, masked_hid, preferred_element_type=jnp.float32).astype(
            jnp.bfloat16
        ),
        "fsdp",
        scatter_dimension=0,
        tiled=True,
    )
    output = lax.psum_scatter(out_total.astype(jnp.bfloat16), "ep", scatter_dimension=1, tiled=True)
    hidden_back = back_total.reshape(row_count, unit_count)
    grad_hidden = (row_prob[:, None] * hidden_back).astype(jnp.bfloat16)
    row_dot = jnp.sum(hidden.astype(jnp.float32) * hidden_back, axis=1)
    prob_terms = valid.astype(jnp.float32) * row_dot[row_of]
    grad_probs = lax.psum(prob_terms, "ep")
    return (output, grad_hidden, grad_weight, grad_probs)


def solution(mesh):
    placed = (
        P("fsdp", "ep"),
        P("fsdp", None, "ep"),
        P("fsdp", None),
        P("fsdp", None),
        P("fsdp", "ep"),
    )
    return jax.shard_map(
        local,
        mesh=mesh,
        in_specs=placed,
        out_specs=(P("fsdp", "ep"), P("fsdp", "ep"), P("fsdp", None, "ep"), P("fsdp", None)),
        check_vma=False,
    )
```

profile of v0, /device:TPU:0, one launch (start us, length us, event | category | flops | bytes accessed | tf_op | source)
XLA Modules:
  0.0 635.5 jit_solution(14992355778642910269)
XLA Ops:
  7.9 8.4 %copy.21 = bf16[768,2,2048]{2,0,1:T(8,128)(2,1)} copy(bf16[768,2,2048]{2,1,0:T(2,128)(2,1)} %param.6) | data formatting | bytes 12582912 | tf_op args[1]
  23.5 25.9 %all-gather.5.cloned.1.call-done = bf16[128,6144]{1,0:T(8,128)(2,1)} async-done(((bf16[128,1536]{1,0:T(8,128)(2,1)}), bf16[128,6144]{1,0:T(8,128)(2,1)}) %all-gather.5.cloned.1.call-update) | async-done | bytes 1572880 | tf_op jit(solution)/shard_map/all_gather | solution.py:46
  49.4 7.1 %gather_fusion.1 = bf16[256,6144]{1,0:T(8,128)(2,1)S(1)} fusion(bf16[128,6144]{1,0:T(8,128)(2,1)} %all-gather.5.cloned.1.call-done, s32[1024]{0:T(1024)S(1)} %pad_clamp_fusion), kind=kCustom, calls=%fused_computation.1 | custom fusion | bytes 6292480 | tf_op jit(solution)/shard_map/gather | solution.py:48
  56.5 24.9 %convolution_convert_fusion = bf16[6144,2,2048]{2,0,1:T(8,128)(2,1)} fusion(bf16[256,6144]{1,0:T(8,128)(2,1)S(1)} %gather_fusion.1, f32[256]{0:T(256)S(1)} %scatter_custom_fusion, pred[256]{0:T(512)(128)(4,1)S(1)} %broadcast_compare_fusion, bf16[256,2]{0,1:T(2,128)(2,1)S(1)} %compare_convert_fusion, bf16[256,2048]{1,0:T(8,128)(2,1)} %param.5), kind=kOutput, calls=%fused_computation.31 | convolution fusion | flops 12920553472 | bytes 54528256 | tf_op jit(solution)/shard_map/rd,rei->dei/dot_general | solution.py:70
  83.2 199.5 %all-gather.3.cloned.1.call-done = bf16[6144,2,2048]{2,0,1:T(8,128)(2,1)} async-done(((bf16[768,2,2048]{2,0,1:T(8,128)(2,1)}), bf16[6144,2,2048]{2,0,1:T(8,128)(2,1)}) %all-gather.3.cloned.1.call-update) | async-done | bytes 50331664 | tf_op jit(solution)/shard_map/all_gather | solution.py:57
  282.7 41.5 %fusion.28 = (bf16[512,2,2048]{2,0,1:T(8,128)(2,1)}, bf16[512,2,2048]{2,0,1:T(8,128)(2,1)}, bf16[512,2,2048]{2,0,1:T(8,128)(2,1)}, bf16[512,2,2048]{2,0,1:T(8,12...) fusion(bf16[6144,2,2048]{2,0,1:T(8,128)(2,1)} %all-gather.3.clo, ...), kind=kLoop, calls=%fused_computation.108 | loop fusion | bytes 100663296 | tf_op jit(solution)/shard_map/jit(_take)/gather | solution.py:59
  327.2 9.6 %while.12 = (s32[]{:T(128)}, bf16[512,2,2048]{2,0,1:T(8,128)(2,1)}, s32[2,1]{0,1:T(1,128)S(1)}, bf16[2,512,2048]{2,1,0:T(8,128)(2,1)}, s32[]{:T(128)}) while((s32[]{:T(128)}, bf16[512,2,2048]{2,0,1:T(8,128)(2,1)}, s32[2,1]{0,1:T(1,128)S(1)}, bf16[2,512,2048]{2,1,0:T(8,128)(2,1)}, s32[]{:T(128)}) %tuple.161), condition=%wide.while_cond, body=%wide.while_body.sunk | while | flops 2 | bytes 4195401 | solution.py:59
  327.8 4.2 bitcast_dynamic-update-slice_fusion.36
  332.5 4.3 bitcast_dynamic-update-slice_fusion.36
  339.9 9.5 %while.13 = (s32[]{:T(128)}, bf16[512,2,2048]{2,0,1:T(8,128)(2,1)}, s32[2,1]{0,1:T(1,128)S(1)}, bf16[2,512,2048]{2,1,0:T(8,128)(2,1)}, s32[]{:T(128)}) while((s32[]{:T(128)}, bf16[512,2,2048]{2,0,1:T(8,128)(2,1)}, s32[2,1]{0,1:T(1,128)S(1)}, bf16[2,512,2048]{2,1,0:T(8,128)(2,1)}, s32[]{:T(128)}) %tuple.205), condition=%wide.while_cond.1, body=%wide.while_body.1.sunk | while | flops 2 | bytes 4195401 | solution.py:59
  340.5 4.3 bitcast_dynamic-update-slice_fusion.37
  352.0 8.8 %while.14 = (s32[]{:T(128)}, bf16[512,2,2048]{2,0,1:T(8,128)(2,1)}, s32[2,1]{0,1:T(1,128)S(1)}, bf16[2,512,2048]{2,1,0:T(8,128)(2,1)}, s32[]{:T(128)}) while((s32[]{:T(128)}, bf16[512,2,2048]{2,0,1:T(8,128)(2,1)}, s32[2,1]{0,1:T(1,128)S(1)}, bf16[2,512,2048]{2,1,0:T(8,128)(2,1)}, s32[]{:T(128)}) %tuple.206), condition=%wide.while_cond.2, body=%wide.while_body.2.sunk | while | flops 2 | bytes 4195401 | solution.py:59
  363.4 9.2 %while.15 = (s32[]{:T(128)}, bf16[512,2,2048]{2,0,1:T(8,128)(2,1)}, s32[2,1]{0,1:T(1,128)S(1)}, bf16[2,512,2048]{2,1,0:T(8,128)(2,1)}, s32[]{:T(128)}) while((s32[]{:T(128)}, bf16[512,2,2048]{2,0,1:T(8,128)(2,1)}, s32[2,1]{0,1:T(1,128)S(1)}, bf16[2,512,2048]{2,1,0:T(8,128)(2,1)}, s32[]{:T(128)}) %tuple.207), condition=%wide.while_cond.3, body=%wide.while_body.3.sunk | while | flops 2 | bytes 4195401 | solution.py:59
  375.1 9.1 %while.16 = (s32[]{:T(128)}, bf16[512,2,2048]{2,0,1:T(8,128)(2,1)}, s32[2,1]{0,1:T(1,128)S(1)}, bf16[2,512,2048]{2,1,0:T(8,128)(2,1)}, s32[]{:T(128)}) while((s32[]{:T(128)}, bf16[512,2,2048]{2,0,1:T(8,128)(2,1)}, s32[2,1]{0,1:T(1,128)S(1)}, bf16[2,512,2048]{2,1,0:T(8,128)(2,1)}, s32[]{:T(128)}) %tuple.208), condition=%wide.while_cond.4, body=%wide.while_body.4.sunk | while | flops 2 | bytes 4195401 | solution.py:59
  386.7 8.8 %while.17 = (s32[]{:T(128)}, bf16[512,2,2048]{2,0,1:T(8,128)(2,1)}, s32[2,1]{0,1:T(1,128)S(1)}, bf16[2,512,2048]{2,1,0:T(8,128)(2,1)}, s32[]{:T(128)}) while((s32[]{:T(128)}, bf16[512,2,2048]{2,0,1:T(8,128)(2,1)}, s32[2,1]{0,1:T(1,128)S(1)}, bf16[2,512,2048]{2,1,0:T(8,128)(2,1)}, s32[]{:T(128)}) %tuple.209), condition=%wide.while_cond.5, body=%wide.while_body.5.sunk | while | flops 2 | bytes 4195401 | solution.py:59
  398.1 8.8 %while.18 = (s32[]{:T(128)}, bf16[512,2,2048]{2,0,1:T(8,128)(2,1)}, s32[2,1]{0,1:T(1,128)S(1)}, bf16[2,512,2048]{2,1,0:T(8,128)(2,1)}, s32[]{:T(128)}) while((s32[]{:T(128)}, bf16[512,2,2048]{2,0,1:T(8,128)(2,1)}, s32[2,1]{0,1:T(1,128)S(1)}, bf16[2,512,2048]{2,1,0:T(8,128)(2,1)}, s32[]{:T(128)}) %tuple.210), condition=%wide.while_cond.6, body=%wide.while_body.6.sunk | while | flops 2 | bytes 4195401 | solution.py:59
  409.4 9.3 %while.19 = (s32[]{:T(128)}, bf16[512,2,2048]{2,0,1:T(8,128)(2,1)}, s32[2,1]{0,1:T(1,128)S(1)}, bf16[2,512,2048]{2,1,0:T(8,128)(2,1)}, s32[]{:T(128)}) while((s32[]{:T(128)}, bf16[512,2,2048]{2,0,1:T(8,128)(2,1)}, s32[2,1]{0,1:T(1,128)S(1)}, bf16[2,512,2048]{2,1,0:T(8,128)(2,1)}, s32[]{:T(128)}) %tuple.211), condition=%wide.while_cond.7, body=%wide.while_body.7.sunk | while | flops 2 | bytes 4195401 | solution.py:59
  410.0 4.2 bitcast_dynamic-update-slice_fusion.43
  421.2 8.8 %while.20 = (s32[]{:T(128)}, bf16[512,2,2048]{2,0,1:T(8,128)(2,1)}, s32[2,1]{0,1:T(1,128)S(1)}, bf16[2,512,2048]{2,1,0:T(8,128)(2,1)}, s32[]{:T(128)}) while((s32[]{:T(128)}, bf16[512,2,2048]{2,0,1:T(8,128)(2,1)}, s32[2,1]{0,1:T(1,128)S(1)}, bf16[2,512,2048]{2,1,0:T(8,128)(2,1)}, s32[]{:T(128)}) %tuple.212), condition=%wide.while_cond.8, body=%wide.while_body.8.sunk | while | flops 2 | bytes 4195401 | solution.py:59
  432.5 8.7 %while.21 = (s32[]{:T(128)}, bf16[512,2,2048]{2,0,1:T(8,128)(2,1)}, s32[2,1]{0,1:T(1,128)S(1)}, bf16[2,512,2048]{2,1,0:T(8,128)(2,1)}, s32[]{:T(128)}) while((s32[]{:T(128)}, bf16[512,2,2048]{2,0,1:T(8,128)(2,1)}, s32[2,1]{0,1:T(1,128)S(1)}, bf16[2,512,2048]{2,1,0:T(8,128)(2,1)}, s32[]{:T(128)}) %tuple.213), condition=%wide.while_cond.9, body=%wide.while_body.9.sunk | while | flops 2 | bytes 4195401 | solution.py:59
  443.9 8.9 %while.22 = (s32[]{:T(128)}, bf16[512,2,2048]{2,0,1:T(8,128)(2,1)}, s32[2,1]{0,1:T(1,128)S(1)}, bf16[2,512,2048]{2,1,0:T(8,128)(2,1)}, s32[]{:T(128)}) while((s32[]{:T(128)}, bf16[512,2,2048]{2,0,1:T(8,128)(2,1)}, s32[2,1]{0,1:T(1,128)S(1)}, bf16[2,512,2048]{2,1,0:T(8,128)(2,1)}, s32[]{:T(128)}) %tuple.214), condition=%wide.while_cond.10, body=%wide.while_body.10.sunk | while | flops 2 | bytes 4195401 | solution.py:59
  455.3 9.4 %while.23 = (s32[]{:T(128)}, bf16[512,2,2048]{2,0,1:T(8,128)(2,1)}, s32[2,1]{0,1:T(1,128)S(1)}, bf16[2,512,2048]{2,1,0:T(8,128)(2,1)}, s32[]{:T(128)}) while((s32[]{:T(128)}, bf16[512,2,2048]{2,0,1:T(8,128)(2,1)}, s32[2,1]{0,1:T(1,128)S(1)}, bf16[2,512,2048]{2,1,0:T(8,128)(2,1)}, s32[]{:T(128)}) %tuple.215), condition=%wide.while_cond.11, body=%wide.while_body.11.sunk | while | flops 2 | bytes 4195401 | solution.py:59
  460.6 4.2 bitcast_dynamic-update-slice_fusion.47
  464.7 5.3 bitcast_dynamic-update-slice_fusion.23
  510.1 25.9 %fusion.1 = f32[2,6144,128]{1,2,0:T(8,128)} fusion(bf16[2,128,2048]{2,1,0:T(8,128)(2,1)S(1)} %bitcast.149, bf16[6144,2,2048]{2,0,1:T(8,128)(2,1)} %bitcast_dynamic-update-slice_fusion.12, pred[2]{0:T(512)(128)(4,1)S(1)} %maximum_compare_fusion), kind=kOutput, calls=%fused_computation.33 | convolution fusion | flops 6467616768 | bytes 57671680 | tf_op jit(solution)/shard_map/bri,dbi->brd/dot_general | solution.py:60
  536.0 10.6 %gather_fusion = f32[256,6144]{1,0:T(8,128)} fusion(f32[256,6144]{1,0:T(8,128)} %bitcast.147, s32[1024]{0:T(1024)S(1)} %copy-done.14), kind=kCustom, calls=%fused_computation | custom fusion | bytes 12583936 | tf_op jit(solution)/shard_map/gather | solution.py:66
  546.6 8.4 %reshape.505 = f32[128,2,6144]{2,1,0:T(2,128)} reshape(f32[256,6144]{1,0:T(8,128)} %gather_fusion) | data formatting | bytes 12582912 | tf_op jit(solution)/shard_map/gather | solution.py:66
  555.0 20.2 %fusion = f32[2,128,2048]{2,1,0:T(8,128)} fusion(bf16[6144,2,2048]{2,0,1:T(8,128)(2,1)} %bitcast_dynamic-update-slice_fusion.12, pred[2]{0:T(512)(128)(4,1)S(1)} %maximum_compare_fusion, bf16[2,128,6144]{2,1,0:T(8,128)(2,1)S(1)} %bitcast.148, pred[2,128]{1,0:T(4,128)(4,1)S(1)} %copy-done.22), kind=kOutput, calls=%fused_computation.32 | convolution fusion | flops 6469189632 | bytes 55574784 | tf_op jit(solution)/shard_map/brd,dbi->bri/dot_general | solution.py:63
  581.0 11.9 %multiply_reduce_fusion = bf16[128,6144]{1,0:T(8,128)(2,1)} fusion(f32[128,2,6144]{2,1,0:T(2,128)} %reshape.505, f32[128,2]{1,0:T(8,128)S(1)} %copy.20), kind=kLoop, calls=%fused_computation.35 | loop fusion | flops 2359296 | bytes 7865344 | tf_op jit(solution)/shard_map/reduce_sum | solution.py:66
  592.9 12.6 %copy.30 = bf16[768,2,2048]{2,1,0:T(2,128)(2,1)} copy(bf16[768,2,2048]{2,0,1:T(8,128)(2,1)} %reduce-scatter.5.cloned.1.call-done) | data formatting | bytes 12582912
  605.5 12.9 %psum.7 = f32[128,2]{0,1:T(2,128)} all-reduce(f32[128,2]{0,1:T(2,128)S(1)} %get-tuple-element.225), channel_id=1, replica_groups=mesh['fsdp'=8,'ep'=4] {'ep'}, use_global_device_ids=true, to_apply=%region_14.15 | all-reduce | flops 256 | bytes 2048 | tf_op jit(solution)/shard_map/psum | solution.py:82
  618.5 10.2 %reduce-scatter.3.cloned.1.call-done = bf16[128,1536]{1,0:T(8,128)(2,1)} async-done(((bf16[128,6144]{1,0:T(8,128)(2,1)}), bf16[128,1536]{1,0:T(8,128)(2,1)}) %reduce-scatter.3.cloned.1.call-update) | async-done | bytes 393232 | tf_op jit(solution)/shard_map/reduce_scatter | solution.py:77
  (162 shorter events, 174.6 us)
Async XLA Ops:
  7.2 42.2 %all-gather.5.cloned.1.call-start = ((), (), s32[]{:S(2)}) async-start(), calls=%async_computation.4 | async-start | bytes 1966080 | tf_op jit(solution)/shard_map/all_gather | solution.py:46
  7.9 274.8 %all-gather.3.cloned.1.call-start = ((), (), s32[]{:S(2)}) async-start(), calls=%async_computation.2 | async-start | bytes 56623104 | tf_op jit(solution)/shard_map/all_gather | solution.py:57
  16.3 0.7 copy-start.21
  16.3 4.7 copy-start.19
  16.4 576.5 %reduce-scatter.5.cloned.1.call-start = ((), (), s32[]{:S(2)}) async-start(), calls=%async_computation.5 | async-start | bytes 56623104 | tf_op jit(solution)/shard_map/reduce_scatter | solution.py:69
  17.1 6.4 %copy-start.17 = (s32[128,2]{0,1:T(2,128)}, s32[128,2]{0,1:T(2,128)S(1)}, u32[]{:S(2)}) copy-start(s32[128,2]{0,1:T(2,128)S(1)} %get-tuple-element.112) | copy-start | bytes 3076
  23.2 33.3 %copy-start.15 = (f32[256]{0:T(256)}, f32[256]{0:T(256)S(1)}, u32[]{:S(2)}) copy-start(f32[256]{0:T(256)S(1)} %scatter_custom_fusion) | copy-start | bytes 3076
  56.5 25.0 %copy-start.11 = (bf16[256,6144]{1,0:T(8,128)(2,1)}, bf16[256,6144]{1,0:T(8,128)(2,1)S(1)}, u32[]{:S(2)}) copy-start(bf16[256,6144]{1,0:T(8,128)(2,1)S(1)} %gather_fusion.1) | copy-start | bytes 9437188
  81.5 547.2 %reduce-scatter.3.cloned.1.call-start = ((), (), s32[]{:S(2)}) async-start(), calls=%async_computation.3 | async-start | bytes 1966080 | tf_op jit(solution)/shard_map/reduce_scatter | solution.py:77
  464.7 5.3 copy-start.1
  470.0 3.8 copy-start.2
  473.9 3.9 copy-start.3
  477.7 3.9 copy-start.4
  481.6 3.7 copy-start.5
  485.3 3.7 copy-start.6
  489.0 3.7 copy-start.7
  492.8 3.7 copy-start.8
  496.5 3.7 copy-start.9
  500.2 4.0 copy-start.10
  504.2 3.7 copy-start
  507.9 2.2 copy-start.13
  510.1 25.9 %copy-start.14 = (s32[1024]{0:T(1024)S(1)}, s32[1024]{0:T(1024)}, u32[]{:S(2)}) copy-start(s32[1024]{0:T(1024)} %pad_clamp_fusion.1) | copy-start | bytes 12292
  546.6 8.4 %copy-start.12 = (bf16[256,6144]{1,0:T(8,128)(2,1)S(1)}, bf16[256,6144]{1,0:T(8,128)(2,1)}, u32[]{:S(2)}) copy-start(bf16[256,6144]{1,0:T(8,128)(2,1)} %copy-done.11) | copy-start | bytes 9437188
  546.6 8.4 %copy-start.22 = (pred[2,128]{1,0:T(4,128)(4,1)S(1)}, pred[2,128]{1,0:T(4,128)(4,1)}, u32[]{:S(2)}) copy-start(pred[2,128]{1,0:T(4,128)(4,1)} %fusion.30) | copy-start | bytes 772
  555.0 20.2 %copy-start.16 = (f32[256]{0:T(256)S(1)}, f32[256]{0:T(256)}, u32[]{:S(2)}) copy-start(f32[256]{0:T(256)} %copy-done.15) | copy-start | bytes 3076
  578.4 2.4 copy-start.18
  578.4 2.4 copy-start.20
Sparse Core Ops, SparseCore 0:
  9.6 39.7 all-gather.4
  51.9 230.7 all-gather.2
  286.3 285.8 reduce-scatter.4
  593.0 35.6 reduce-scatter.2
where the time goes:
time: 642 us; the launch traced here: 635 us
  local copies, waits for them, and re-layouts  283 us (44%)
  waiting for transfers between devices  236 us (37%)
  matrix products  71.1 us (11%)
  other arithmetic  17 us (3%)
  between operations  14.3 us (2%)
  blocking collectives  12.9 us (2%)
    all_gather x1, waiting for transfers between devices, local(): piece = lax.all_gather(w_down, 'fsdp', axis=0, tiled=True)  200 us
    gather x48, local copies, waits for them, and re-layouts  109 us
    unnamed x73, local copies, waits for them, and re-layouts  98.7 us
    gather x1, local copies, waits for them, and re-layouts, local(): chosen = jnp.take(piece, safe_exp, axis=1)  41.5 us
    dot_general x1, matrix products, local(): jnp.einsum('bri,dbi->brd', hid_blocks, chosen, preferred_element_type=jnp...  25.9 us
    all_gather x1, waiting for transfers between devices, local(): full_grads = lax.all_gather(grad_out, 'ep', axis=1, tiled=True)  25.9 us
    dot_general x1, matrix products, local(): jnp.einsum('rd,rei->dei', scaled, masked_hid, preferred_element_type=jnp....  24.9 us
    dot_general x1, matrix products, local(): jnp.einsum('brd,dbi->bri', routed_blocks, chosen, preferred_element_type=...  20.2 us
  transfers between devices with their start and end apart: 4, of which 3 were waited for; matrix products, arithmetic and copies ran while one was open for 56% of the time, Pallas kernels for 0%

commit v1 on v0

--- a/solution.py
+++ b/solution.py
@@ -4,6 +4,12 @@
 from jax.sharding import PartitionSpec as P
 
 BLOCK = 128
+
+
+def laid_out(blocks, dim):
+    blocks = jnp.moveaxis(blocks, 0, dim)
+    shape = blocks.shape
+    return blocks.reshape(*shape[:dim], shape[dim] * shape[dim + 1], *shape[dim + 2 :])
 
 
 def route_layout(route_part, prob_part, expert_count, block_rows, row_count):
@@ -54,7 +60,19 @@
         jnp.bfloat16
     )
     masked_hid = hidden[:, None, :] * member[:, :, None]
-    piece = lax.all_gather(w_down, "fsdp", axis=0, tiled=True)
+    count = lax.axis_size("fsdp")
+    pairs = [(i, (i + 1) % count) for i in range(count)]
+    back = [(b, a) for a, b in pairs]
+    lower, upper = ([], [])
+    for step in range(count - 1):
+        if step % 2 == 0:
+            lower.append(lax.ppermute(lower[-1] if lower else w_down, "fsdp", pairs))
+        else:
+            upper.append(lax.ppermute(upper[-1] if upper else w_down, "fsdp", back))
+    tiles = jnp.stack([*lower[::-1], w_down, *upper])
+    shift = lax.axis_index("fsdp") - len(lower)
+    tiles = tiles[(jnp.arange(count) - shift) % count]
+    piece = laid_out(tiles, 0)
     width = piece.shape[0]
     chosen = jnp.take(piece, safe_exp, axis=1)
     out_rows = jnp.einsum(

time: 642 us -> 1320 us (2.06)
  waiting for transfers between devices: 236 us -> 623 us
  local copies, waits for them, and re-layouts: 283 us -> 516 us
  other arithmetic: 17 us -> 71.1 us
    ppermute x0 -> x7, waiting for transfers between devices: none -> 579 us  [the longest x4 395 us: local(): lower.append(lax.ppermute(lower[-1] if lower else w_down, 'fsdp', pairs))]
    all_gather x1 -> x0, waiting for transfers between devices: 200 us -> none  [local(): piece = lax.all_gather(w_down, 'fsdp', axis=0, tiled=True)]
    gather x48 -> x53, local copies, waits for them, and re-layouts: 109 us -> 277 us  [the longest x5 171 us: local(): tiles = tiles[(jnp.arange(count) - shift) % count]]
    unnamed x73 -> x84, local copies, waits for them, and re-layouts: 98.7 us -> 168 us
    unnamed x0 -> x2, other arithmetic: none -> 51.7 us
  transfers between devices with their start and end apart: 4 -> 10, of which waited for: 3 -> 8; matrix products, arithmetic and copies ran while one was open for 56% -> 49% of each run, Pallas kernels for 0% -> 0%
where the time goes in v1:
time: 1320 us; the launch traced here: 1310 us
  waiting for transfers between devices  623 us (47%)
  local copies, waits for them, and re-layouts  516 us (39%)
  other arithmetic  71.1 us (5%)
  matrix products  66.2 us (5%)
  between operations  14.5 us (1%)
  blocking collectives  14.2 us (1%)
    ppermute x4, waiting for transfers between devices, local(): lower.append(lax.ppermute(lower[-1] if lower else w_down, 'fsdp', pairs))  395 us
    ppermute x3, waiting for transfers between devices, local(): upper.append(lax.ppermute(upper[-1] if upper else w_down, 'fsdp', back))  184 us
    gather x5, local copies, waits for them, and re-layouts, local(): tiles = tiles[(jnp.arange(count) - shift) % count]  171 us
    unnamed x84, local copies, waits for them, and re-layouts  168 us
    gather x48, local copies, waits for them, and re-layouts  105 us
    unnamed x2, other arithmetic  51.7 us
    gather x1, local copies, waits for them, and re-layouts, local(): chosen = jnp.take(piece, safe_exp, axis=1)  33.2 us
    all_gather x1, waiting for transfers between devices, local(): full_grads = lax.all_gather(grad_out, 'ep', axis=1, tiled=True)  32.9 us
  transfers between devices with their start and end apart: 10, of which 8 were waited for; matrix products, arithmetic and copies ran while one was open for 49% of the time, Pallas kernels for 0%

profile of v1, /device:TPU:0, one launch (start us, length us, event | category | flops | bytes accessed | tf_op | source)
XLA Modules:
  0.0 1314.8 jit_solution(17388387631375160824)
XLA Ops:
  16.5 32.9 %all-gather.2.cloned.1.call-done = bf16[128,6144]{1,0:T(8,128)(2,1)} async-done(((bf16[128,1536]{1,0:T(8,128)(2,1)}), bf16[128,6144]{1,0:T(8,128)(2,1)}) %all-gather.2.cloned.1.call-update) | async-done | bytes 1572880 | tf_op jit(solution)/shard_map/all_gather | solution.py:52
  56.5 23.1 %collective-permute-done = bf16[768,2,2048]{2,1,0:T(2,128)(2,1)} collective-permute-done((bf16[768,2,2048]{2,1,0:T(2,128)(2,1)}, bf16[768,2,2048]{2,1,0:T(2,128)(2,1)}, u32[]{:S(2)}, u32[]{:S(2)}) %collective-permute-start) | collective-permute-done | bytes 6291488 | tf_op jit(solution)/shard_map/ppermute | solution.py:69
  79.8 21.7 %convolution_convert_fusion = bf16[6144,2,2048]{2,0,1:T(8,128)(2,1)} fusion(bf16[256,6144]{1,0:T(8,128)(2,1)S(1)} %gather_fusion.1, f32[256]{0:T(256)S(1)} %scatter_custom_fusion, pred[256]{0:T(512)(128)(4,1)S(1)} %broadcast_compare_fusion, bf16[256,2]{0,1:T(2,128)(2,1)S(1)} %compare_convert_fusion, bf16[256,2048]{1,0:T(8,128)(2,1)} %param.5), kind=kOutput, calls=%fused_computation.36 | convolution fusion | flops 12920553472 | bytes 54528256 | tf_op jit(solution)/shard_map/rd,rei->dei/dot_general | solution.py:88
  104.3 105.6 %collective-permute-done.1 = bf16[768,2,2048]{2,1,0:T(2,128)(2,1)} collective-permute-done((bf16[768,2,2048]{2,1,0:T(2,128)(2,1)}, bf16[768,2,2048]{2,1,0:T(2,128)(2,1)}, u32[]{:S(2)}, u32[]{:S(2)}) %collective-permute-start.1) | collective-permute-done | bytes 6291488 | tf_op jit(solution)/shard_map/ppermute | solution.py:69
  209.9 92.6 %collective-permute-done.4 = bf16[768,2,2048]{2,1,0:T(2,128)(2,1)} collective-permute-done((bf16[768,2,2048]{2,1,0:T(2,128)(2,1)}, bf16[768,2,2048]{2,1,0:T(2,128)(2,1)}, u32[]{:S(2)}, u32[]{:S(2)}) %collective-permute-start.4) | collective-permute-done | bytes 6291488 | tf_op jit(solution)/shard_map/ppermute | solution.py:71
  305.3 167.9 %collective-permute-done.2 = bf16[768,2,2048]{2,1,0:T(2,128)(2,1)} collective-permute-done((bf16[768,2,2048]{2,1,0:T(2,128)(2,1)}, bf16[768,2,2048]{2,1,0:T(2,128)(2,1)}, u32[]{:S(2)}, u32[]{:S(2)}) %collective-permute-start.2) | collective-permute-done | bytes 6291488 | tf_op jit(solution)/shard_map/ppermute | solution.py:69
  475.1 90.9 %collective-permute-done.5 = bf16[768,2,2048]{2,1,0:T(2,128)(2,1)} collective-permute-done((bf16[768,2,2048]{2,1,0:T(2,128)(2,1)}, bf16[768,2,2048]{2,1,0:T(2,128)(2,1)}, u32[]{:S(2)}, u32[]{:S(2)}) %collective-permute-start.5) | collective-permute-done | bytes 6291488 | tf_op jit(solution)/shard_map/ppermute | solution.py:71
  568.9 98.7 %collective-permute-done.3 = bf16[768,2,2048]{2,1,0:T(2,128)(2,1)} collective-permute-done((bf16[768,2,2048]{2,1,0:T(2,128)(2,1)}, bf16[768,2,2048]{2,1,0:T(2,128)(2,1)}, u32[]{:S(2)}, u32[]{:S(2)}) %collective-permute-start.3) | collective-permute-done | bytes 6291488 | tf_op jit(solution)/shard_map/ppermute | solution.py:69
  719.5 38.3 %fusion.31 = (bf16[8,768,2,512]{3,2,1,0:T(2,128)(2,1)}, bf16[8,768,2,512]{3,2,1,0:T(2,128)(2,1)}, bf16[8,768,2,512]{3,2,1,0:T(2,128)(2,1)}, bf16[8,768,2,512]{3,2,1,0:T(2,128)(2,1)}) fusion(bf16[8,768,2,2048]{3,2,1,0:T(2,128)(2,1)} %bitcast_dynamic-update-slice_fusion.12), kind=kLoop, calls=%fused_computation.129 | loop fusion | bytes 100663296 | tf_op jit(solution)/shard_map/gather | solution.py:74
  757.8 31.0 %gather_fusion.3 = bf16[8,768,2,512]{3,2,1,0:T(2,128)(2,1)} fusion(bf16[8,768,2,512]{3,2,1,0:T(2,128)(2,1)} %get-tuple-element.223, s32[1024]{0:T(1024)S(1)} %get-tuple-element.234), kind=kCustom, calls=%fused_computation.3 | custom fusion | bytes 25165856 | tf_op jit(solution)/shard_map/gather | solution.py:74
  788.8 31.0 %gather_fusion.4 = bf16[8,768,2,512]{3,2,1,0:T(2,128)(2,1)} fusion(bf16[8,768,2,512]{3,2,1,0:T(2,128)(2,1)} %get-tuple-element.225, s32[1024]{0:T(1024)S(1)} %get-tuple-element.234), kind=kCustom, calls=%fused_computation.4 | custom fusion | bytes 25165856 | tf_op jit(solution)/shard_map/gather | solution.py:74
  819.8 39.7 %gather_fusion.5 = bf16[8,768,2,512]{3,2,1,0:T(2,128)(2,1)} fusion(bf16[8,768,2,512]{3,2,1,0:T(2,128)(2,1)} %get-tuple-element.224, s32[1024]{0:T(1024)S(1)} %get-tuple-element.234), kind=kCustom, calls=%fused_computation.5 | custom fusion | bytes 25165856 | tf_op jit(solution)/shard_map/gather | solution.py:74
  859.6 31.0 %gather_fusion.6 = bf16[8,768,2,512]{3,2,1,0:T(2,128)(2,1)} fusion(bf16[8,768,2,512]{3,2,1,0:T(2,128)(2,1)} %get-tuple-element.226, s32[1024]{0:T(1024)S(1)} %get-tuple-element.234), kind=kCustom, calls=%fused_computation.6 | custom fusion | bytes 25165856 | tf_op jit(solution)/shard_map/gather | solution.py:74
  890.6 51.7 %pad_maximum_fusion = bf16[8,768,2,2048]{3,2,1,0:T(2,128)(2,1)} fusion(bf16[8,768,2,512]{3,2,1,0:T(2,128)(2,1)} %gather_fusion.6, bf16[8,768,2,512]{3,2,1,0:T(2,128)(2,1)} %gather_fusion.5, bf16[8,768,2,512]{3,2,1,0:T(2,128)(2,1)} %gather_fusion.4, bf16[8,768,2,512]{3,2,1,0:T(2,128)(2,1)} %gather_fusion.3), kind=kLoop, calls=%fused_computation.34 | loop fusion | flops 201326592 | bytes 100663296
  942.3 33.4 %copy.21 = bf16[8,768,2,2048]{3,1,0,2:T(8,128)(2,1)} copy(bf16[8,768,2,2048]{3,2,1,0:T(2,128)(2,1)} %pad_maximum_fusion) | data formatting | bytes 100663296
  975.7 33.2 %fusion.30 = (bf16[512,2,2048]{2,0,1:T(8,128)(2,1)}, bf16[512,2,2048]{2,0,1:T(8,128)(2,1)}, bf16[512,2,2048]{2,0,1:T(8,128)(2,1)}, bf16[512,2,2048]{2,0,1:T(8,12...) fusion(bf16[6144,2,2048]{2,0,1:T(8,128)(2,1)} %bitcast.167), kind=kLoop, calls=%fused_computation.128 | loop fusion | bytes 100663296 | tf_op jit(solution)/shard_map/jit(_take)/gather | solution.py:77
  1022.4 8.9 while.13
  1033.7 8.8 while.14
  1045.1 8.8 while.15
  1056.3 9.0 while.16
  1067.8 8.8 while.17
  1079.2 8.8 while.18
  1101.8 8.8 while.20
  1113.0 8.8 while.21
  1124.5 8.8 while.22
  1188.8 25.0 %fusion.1 = f32[2,6144,128]{1,2,0:T(8,128)} fusion(bf16[2,128,2048]{2,1,0:T(8,128)(2,1)S(1)} %bitcast.169, bf16[6144,2,2048]{2,0,1:T(8,128)(2,1)} %bitcast_dynamic-update-slice_fusion.20, pred[2]{0:T(512)(128)(4,1)S(1)} %copy-done.22), kind=kOutput, calls=%fused_computation.38 | convolution fusion | flops 6467616768 | bytes 57671680 | tf_op jit(solution)/shard_map/bri,dbi->brd/dot_general | solution.py:78
  1213.8 10.6 gather_fusion
  1232.7 19.5 %fusion = f32[2,128,2048]{2,1,0:T(8,128)} fusion(bf16[6144,2,2048]{2,0,1:T(8,128)(2,1)} %bitcast_dynamic-update-slice_fusion.20, pred[2]{0:T(512)(128)(4,1)S(1)} %copy-done.22, bf16[2,128,6144]{2,1,0:T(8,128)(2,1)S(1)} %bitcast.168, pred[2,128]{1,0:T(4,128)(4,1)S(1)} %copy-done.21), kind=kOutput, calls=%fused_computation.37 | convolution fusion | flops 6469189632 | bytes 55574784 | tf_op jit(solution)/shard_map/brd,dbi->bri/dot_general | solution.py:81
  1257.6 11.9 multiply_reduce_fusion
  1269.5 14.2 %psum.7 = f32[128,2]{0,1:T(2,128)} all-reduce(f32[128,2]{0,1:T(2,128)S(1)} %get-tuple-element.229), channel_id=1, replica_groups=mesh['fsdp'=8,'ep'=4] {'ep'}, use_global_device_ids=true, to_apply=%region_14.15 | all-reduce | flops 256 | bytes 2048 | tf_op jit(solution)/shard_map/psum | solution.py:100
  1283.7 12.6 copy.30
  1296.3 11.5 reduce-scatter.3.cloned.1.call-done
  (193 shorter events, 298.2 us)
Async XLA Ops:
  7.2 42.2 %all-gather.2.cloned.1.call-start = ((), (), s32[]{:S(2)}) async-start(), calls=%async_computation.3 | async-start | bytes 1966080 | tf_op jit(solution)/shard_map/all_gather | solution.py:52
  7.2 72.4 %collective-permute-start = (bf16[768,2,2048]{2,1,0:T(2,128)(2,1)}, bf16[768,2,2048]{2,1,0:T(2,128)(2,1)}, u32[]{:S(2)}, u32[]{:S(2)}) collective-permute-start(bf16[768,2,2048]{2,1,0:T(2,128)(2,1)} %param.6), channel_id=1, source_target_pairs={{0,4},{4,8},{8,12},{12,16},{16,20},{20,24},{24,28},{28,0},{1,5},{5... | collective-permute-start | bytes 18874376 | tf_op jit(solution)/shard_map/ppermute | solution.py:69
  7.9 1275.8 %reduce-scatter.5.cloned.1.call-start = ((), (), s32[]{:S(2)}) async-start(), calls=%async_computation.4 | async-start | bytes 56623104 | tf_op jit(solution)/shard_map/reduce_scatter | solution.py:87
  8.8 7.8 copy-start.17
  15.6 64.2 %copy-start.15 = (f32[256]{0:T(256)}, f32[256]{0:T(256)S(1)}, u32[]{:S(2)}) copy-start(f32[256]{0:T(256)S(1)} %scatter_custom_fusion) | copy-start | bytes 3076
  56.5 45.1 %copy-start.11 = (bf16[256,6144]{1,0:T(8,128)(2,1)}, bf16[256,6144]{1,0:T(8,128)(2,1)S(1)}, u32[]{:S(2)}) copy-start(bf16[256,6144]{1,0:T(8,128)(2,1)S(1)} %gather_fusion.1) | copy-start | bytes 9437188
  79.6 130.3 %collective-permute-start.1 = (bf16[768,2,2048]{2,1,0:T(2,128)(2,1)}, bf16[768,2,2048]{2,1,0:T(2,128)(2,1)}, u32[]{:S(2)}, u32[]{:S(2)}) collective-permute-start(bf16[768,2,2048]{2,1,0:T(2,128)(2,1)} %collective-permute-done), channel_id=1, source_target_pairs={{0,4},{4,8},{8,12},{12,16},{16,20},{20,24},{24,28},{28,0},{1,5},{5... | collective-permute-start | bytes 18874376 | tf_op jit(solution)/shard_map/ppermute | solution.py:69
  101.6 1206.3 %reduce-scatter.3.cloned.1.call-start = ((), (), s32[]{:S(2)}) async-start(), calls=%async_computation.2 | async-start | bytes 1966080 | tf_op jit(solution)/shard_map/reduce_scatter | solution.py:95
  101.6 200.9 %collective-permute-start.4 = (bf16[768,2,2048]{2,1,0:T(2,128)(2,1)}, bf16[768,2,2048]{2,1,0:T(2,128)(2,1)}, u32[]{:S(2)}, u32[]{:S(2)}) collective-permute-start(bf16[768,2,2048]{2,1,0:T(2,128)(2,1)} %param.6), channel_id=1, source_target_pairs={{4,0},{8,4},{12,8},{16,12},{20,16},{24,20},{28,24},{0,28},{5,1},{9... | collective-permute-start | bytes 18874376 | tf_op jit(solution)/shard_map/ppermute | solution.py:71
  209.9 263.3 %collective-permute-start.2 = (bf16[768,2,2048]{2,1,0:T(2,128)(2,1)}, bf16[768,2,2048]{2,1,0:T(2,128)(2,1)}, u32[]{:S(2)}, u32[]{:S(2)}) collective-permute-start(bf16[768,2,2048]{2,1,0:T(2,128)(2,1)} %collective-permute-done.1), channel_id=1, source_target_pairs={{0,4},{4,8},{8,12},{12,16},{16,20},{20,24},{24,28},{28,0},{1,5},{5... | collective-permute-start | bytes 18874376 | tf_op jit(solution)/shard_map/ppermute | solution.py:69
  302.5 263.5 %collective-permute-start.5 = (bf16[768,2,2048]{2,1,0:T(2,128)(2,1)}, bf16[768,2,2048]{2,1,0:T(2,128)(2,1)}, u32[]{:S(2)}, u32[]{:S(2)}) collective-permute-start(bf16[768,2,2048]{2,1,0:T(2,128)(2,1)} %collective-permute-done.4), channel_id=1, source_target_pairs={{4,0},{8,4},{12,8},{16,12},{20,16},{24,20},{28,24},{0,28},{5,1},{9... | collective-permute-start | bytes 18874376 | tf_op jit(solution)/shard_map/ppermute | solution.py:71
  473.2 194.3 %collective-permute-start.3 = (bf16[768,2,2048]{2,1,0:T(2,128)(2,1)}, bf16[768,2,2048]{2,1,0:T(2,128)(2,1)}, u32[]{:S(2)}, u32[]{:S(2)}) collective-permute-start(bf16[768,2,2048]{2,1,0:T(2,128)(2,1)} %collective-permute-done.2), channel_id=1, source_target_pairs={{0,4},{4,8},{8,12},{12,16},{16,20},{20,24},{24,28},{28,0},{1,5},{5... | collective-permute-start | bytes 18874376 | tf_op jit(solution)/shard_map/ppermute | solution.py:69
  566.1 148.0 %collective-permute-start.6 = (bf16[768,2,2048]{2,1,0:T(2,128)(2,1)}, bf16[768,2,2048]{2,1,0:T(2,128)(2,1)S(1)}, u32[]{:S(2)}, u32[]{:S(2)}) collective-permute-start(bf16[768,2,2048]{2,1,0:T(2,128)(2,1)} %collective-permute-done.5), channel_id=1, source_target_pairs={{4,0},{8,4},{12,8},{16,12},{20,16},{24,20},{28,24},{0,28},{5,1},{9... | collective-permute-start | bytes 18874376 | tf_op jit(solution)/shard_map/ppermute | solution.py:71
  681.0 14.2 %slice-start = ((s8[6291456]{0:T(1024)(128)(4,1)}), s8[4194304]{0:T(1024)(128)(4,1)S(1)}, s32[]{:S(2)}) async-start(s8[6291456]{0:T(1024)(128)(4,1)} %bitcast.170), calls=%async_computation.5 | async-start | bytes 8388608
  688.3 6.9 slice-start.1
  1008.9 2.5 copy-start.20
  1144.6 4.9 copy-start.1
  1149.5 3.7 copy-start.2
  1153.2 3.7 copy-start.3
  1156.9 3.7 copy-start.4
  1160.6 3.7 copy-start.5
  1164.3 3.7 copy-start.6
  1168.0 3.7 copy-start.7
  1171.7 3.7 copy-start.8
  1175.4 3.7 copy-start.9
  1179.1 3.7 copy-start.10
  1182.8 3.7 copy-start
  1186.5 2.3 copy-start.22
  1188.8 25.1 %copy-start.14 = (s32[1024]{0:T(1024)S(1)}, s32[1024]{0:T(1024)}, u32[]{:S(2)}) copy-start(s32[1024]{0:T(1024)} %get-tuple-element.233) | copy-start | bytes 12292
  1224.4 8.3 copy-start.12
  1224.4 8.3 copy-start.21
  1232.7 19.5 %copy-start.16 = (f32[256]{0:T(256)S(1)}, f32[256]{0:T(256)}, u32[]{:S(2)}) copy-start(f32[256]{0:T(256)} %copy-done.15) | copy-start | bytes 3076
  (3 other events, 6.6 us)
Sparse Core Ops, SparseCore 0:
  9.6 39.7 all-gather.1
  101.7 488.1 reduce-scatter.4
  1269.7 38.1 reduce-scatter.2
